TPU v7x, 128 devices: a whole 4x4x4 slice. The times are simulated.
128 devices in a mesh: gx: 16 (over x, y), gy: 8 (over z, core).
Axes of the slice: x: 4, y: 4, z: 4, core: 2. Of those that a mesh axis runs over, the one named last changes fastest.
Arguments:
- field: float32 [256, 256, 1536], P('gx', 'gy'), may hold values from -24 to 24
- kappa: float32 [256, 256, 1536], P('gx', 'gy'), may hold values from 0.02 to 0.16
- history: float32 [126, 128, 64, 128], P(None, 'gx', 'gy'), may hold values from -2400 to 2400
Outputs:
- field_next: float32 [256, 256, 1536], P('gx', 'gy')
- basis: float32 [128, 128, 64, 128], P(None, 'gx', 'gy')
- factor: float32 [128, 128], replicated
All inputs are finite; a program needn't handle non-finite values.
Results may differ from a plain program's by a relative error of at most 0.00018.
Values sent between devices are 32-bit elements; how exact they have to be, the bound alone decides.
No kernel may reach another device: no remote copies, remote signals or barrier semaphores. Data moves between devices by JAX's collectives and lax.ppermute only.
A program may use at most 192 MiB of HBM per device.

v0:
```python
import jax
import jax.numpy as jnp
from jax import lax
from jax.sharding import PartitionSpec as P


def extended(block, sides, width):
    for axis, dim in sides:
        count = lax.axis_size(axis)
        forward = [(i, i + 1) for i in range(count - 1)]
        backward = [(target, source) for source, target in forward]
        low = lax.ppermute(
            lax.slice_in_dim(block, block.shape[dim] - width, None, axis=dim), axis, forward
        )
        high = lax.ppermute(lax.slice_in_dim(block, 0, width, axis=dim), axis, backward)
        block = jnp.concatenate([low, block, high], axis=dim)
    return block


def advance(field_pad, kappa_pad):
    field_z = jnp.pad(field_pad, ((0, 0), (0, 0), (1, 1)))
    kappa_z = jnp.pad(kappa_pad, ((0, 0), (0, 0), (1, 1)))
    centre = field_z[1:-1, 1:-1, 1:-1]
    kcentre = kappa_z[1:-1, 1:-1, 1:-1]
    places = [
        (slice(2, None), slice(1, -1), slice(1, -1)),
        (slice(None, -2), slice(1, -1), slice(1, -1)),
        (slice(1, -1), slice(2, None), slice(1, -1)),
        (slice(1, -1), slice(None, -2), slice(1, -1)),
        (slice(1, -1), slice(1, -1), slice(2, None)),
        (slice(1, -1), slice(1, -1), slice(None, -2)),
    ]
    change = jnp.zeros_like(centre)
    for place in places:
        change = change + 0.5 * (kcentre + kappa_z[place]) * (field_z[place] - centre)
    return centre + change


def sample(field):
    a, b, c = field.shape
    return field.reshape(a // 2, 2, b // 4, 4, c // 12, 12)[:, 0, :, 0, :, 0]


def body(field, kappa, history):
    both = jnp.stack([field, kappa])
    padded = extended(both, (("gx", 1), ("gy", 2)), 1)
    kappa_pad = padded[1]
    first = advance(padded[0], kappa_pad)
    first_pad = extended(first, (("gx", 0), ("gy", 1)), 1)
    second = advance(first_pad, kappa_pad)
    block = jnp.concatenate([history, sample(first)[None], sample(second)[None]], 0)
    shape = block.shape
    block = block.reshape(shape[0], -1)
    rows_all = block.shape[1] * lax.axis_size("gx") * lax.axis_size("gy")
    gram = jnp.einsum("ar,br->ab", block, block, precision=lax.Precision.HIGHEST) / rows_all
    total = lax.psum(gram, ("gx", "gy"))
    factor = jnp.linalg.cholesky(total).T
    basis = lax.linalg.triangular_solve(factor.T, block, left_side=True, lower=True)
    return (second, basis.reshape(shape), factor)


def solution(mesh):
    placed = (P("gx", "gy", None), P("gx", "gy", None), P(None, "gx", "gy", None))
    return jax.shard_map(
        body,
        mesh=mesh,
        in_specs=placed,
        out_specs=(P("gx", "gy", None), P(None, "gx", "gy", None), P()),
        check_vma=False,
    )
```

profile of v0, /device:TPU:1, one launch (start us, length us, event | category | flops | bytes accessed | tf_op | source)
XLA Modules:
  0.0 410.7 jit_solution(8603581438563554559)
XLA Ops:
  8.7 4.2 %collective-permute-start = (f32[2,1,32,1536]{3,2,1,0:T(8,128)S(1)}, f32[2,1,32,1536]{3,2,1,0:T(8,128)S(1)}, u32[]{:S(2)}, u32[]{:S(2)}) collective-permute-start(f32[2,1,32,1536]{3,2,1,0:T(8,128)S(1)} %get-tuple-element.19), channel_id=1, source_target_pairs={{0,8},{8,16},{16,24},{24,32},{32,40},{40,48},{48,56},{56,64},{64,7... | collective-permute-start | bytes 1179656 | tf_op jit(solution)/shard_map/ppermute | solution.py:12
  14.1 6.5 %collective-permute-done = f32[2,1,32,1536]{3,2,1,0:T(8,128)S(1)} collective-permute-done((f32[2,1,32,1536]{3,2,1,0:T(8,128)S(1)}, f32[2,1,32,1536]{3,2,1,0:T(8,128)S(1)}, u32[]{:S(2)}, u32[]{:S(2)}) %collective-permute-start) | collective-permute-done | bytes 393248 | tf_op jit(solution)/shard_map/ppermute | solution.py:12
  20.6 3.9 collective-permute-done.1
  24.8 5.2 %collective-permute-start.2 = (f32[2,18,1,1536]{3,2,1,0:T(1,128)S(1)}, f32[2,18,1,1536]{3,2,1,0:T(1,128)S(1)}, u32[]{:S(2)}, u32[]{:S(2)}) collective-permute-start(f32[2,18,1,1536]{3,2,1,0:T(1,128)S(1)} %get-tuple-element.17), channel_id=1, source_target_pairs={{0,1},{1,2},{2,3},{3,4},{4,5},{5,6},{6,7},{8,9},{9,10},{10,11},{11... | collective-permute-start | bytes 663560 | tf_op jit(solution)/shard_map/ppermute | solution.py:12
  30.1 1.9 collective-permute-start.3
  32.9 4.4 %collective-permute-done.3 = f32[2,18,1,1536]{3,2,1,0:T(1,128)S(1)} collective-permute-done((f32[2,18,1,1536]{3,2,1,0:T(1,128)S(1)}, f32[2,18,1,1536]{3,2,1,0:T(1,128)S(1)}, u32[]{:S(2)}, u32[]{:S(2)}) %collective-permute-start.3) | collective-permute-done | bytes 221216 | tf_op jit(solution)/shard_map/ppermute | solution.py:15
  37.3 1.7 pad_maximum_fusion
  39.0 4.2 %slice_bitcast_fusion = (f32[18,34,1536]{2,1,0:T(8,128)}, f32[18,34,1536]{2,1,0:T(8,128)}) fusion(f32[2,18,34,1536]{3,2,1,0:T(8,128)S(1)} %pad_maximum_fusion), kind=kLoop, calls=%fused_computation.12 | loop fusion | bytes 15040512 | tf_op jit(solution)/shard_map/squeeze | solution.py:47
  43.2 28.3 %fusion.15 = f32[16,32,1536]{2,1,0:T(8,128)S(1)} fusion(f32[18,34,1536]{2,1,0:T(8,128)} %get-tuple-element.16, f32[18,34,1536]{2,1,0:T(8,128)} %get-tuple-element.15), kind=kLoop, calls=%fused_computation.29 | loop fusion | flops 23592960 | bytes 43450368 | tf_op jit(solution)/shard_map/add | solution.py:36
  71.6 1.6 collective-permute-start.4
  73.1 4.0 collective-permute-start.5
  80.6 1.9 collective-permute-start.6
  83.1 4.0 collective-permute-start.7
  87.2 4.3 %copy.50 = f32[126,8,8,128]{3,0,2,1:T(8,128)} copy(f32[126,8,8,128]{3,2,1,0:T(8,128)S(1)} %copy-done.2) | data formatting | bytes 8257536 | tf_op args[2]
  91.5 5.9 %copy.63 = f32[126,8,8,128]{0,3,2,1:T(8,128)} copy(f32[126,8,8,128]{3,2,1,0:T(8,128)} %param.5) | data formatting | bytes 8257536 | tf_op jit(solution)/shard_map/concatenate | solution.py:51
  97.5 38.1 %reshape.29 = f32[8,2,8,4,128,12]{5,4,3,2,1,0:T(8,128)} reshape(f32[16,32,1536]{2,1,0:T(8,128)S(1)} %fusion.15) | data formatting | bytes 6291456 | tf_op jit(solution)/shard_map/reshape | solution.py:41
  135.6 4.7 %slice.184 = f32[8,1,8,1,128,1]{5,4,3,2,1,0:T(8,128)} slice(f32[8,2,8,4,128,12]{5,4,3,2,1,0:T(8,128)} %reshape.29), slice={[0:8], [0:1], [0:8], [0:1], [0:128], [0:1]} | slice | bytes 65536 | tf_op jit(solution)/shard_map/slice | solution.py:41
  140.3 3.4 copy.64
  143.8 3.3 copy.54
  149.3 4.7 %select_maximum_fusion = f32[18,34,1538]{2,1,0:T(8,128)S(1)} fusion(f32[18,1,1536]{2,1,0:T(1,128)S(1)} %copy.43, f32[18,1,1536]{2,1,0:T(1,128)S(1)} %copy.45, f32[1,32,1536]{2,1,0:T(8,128)S(1)} %collective-permute-done.4, f32[16,32,1536]{2,1,0:T(8,128)S(1)} %fusion.15, f32[1,32,1536]{2,1,0:T(8,128)S(1)} %collective-permute-done.5), kind=kLoop, calls=%fused_computation.3 | loop fusion | flops 11295072 | bytes 7525152 | tf_op jit(solution)/shard_map/concatenate | solution.py:16
  154.0 12.9 %fusion.20 = f32[16,32,1536]{2,1,0:T(8,128)} fusion(f32[16,32,1536]{2,1,0:T(8,128)S(1)} %fusion.15, f32[18,34,1538]{2,1,0:T(8,128)S(1)} %select_maximum_fusion, f32[18,1,1536]{2,1,0:T(1,128)S(1)} %copy.45, f32[1,32,1536]{2,1,0:T(8,128)S(1)} %collective-permute-done.4, f32[1,32,1536]{2,1,0:T(8,128)S(1)} %collective-permute-done.5, ...), kind=kLoop, calls=%fused_computation.35 | loop fusion | flops 29884416 | bytes 33349632 | tf_op jit(solution)/shard_map/add | solution.py:36
  167.0 39.1 %reshape.30 = f32[8,2,8,4,128,12]{5,4,3,2,1,0:T(8,128)} reshape(f32[16,32,1536]{2,1,0:T(8,128)} %fusion.20) | data formatting | bytes 6291456 | tf_op jit(solution)/shard_map/reshape | solution.py:41
  206.1 4.7 %slice.185 = f32[8,1,8,1,128,1]{5,4,3,2,1,0:T(8,128)} slice(f32[8,2,8,4,128,12]{5,4,3,2,1,0:T(8,128)} %reshape.30), slice={[0:8], [0:1], [0:8], [0:1], [0:128], [0:1]} | slice | bytes 65536 | tf_op jit(solution)/shard_map/slice | solution.py:41
  210.8 2.8 copy.65
  213.7 7.7 %fusion.48 = f32[128,128]{0,1:T(8,128)} fusion(f32[1,8,8,128]{3,0,2,1:T(1,128)S(1)} %bitcast.44, f32[1,8,8,128]{3,0,2,1:T(1,128)S(1)} %bitcast.43, f32[126,8,8,128]{3,0,2,1:T(8,128)} %copy.50), kind=kOutput, calls=%fused_computation.78 | convolution fusion | flops 1612726272 | bytes 4259840 | tf_op jit(solution)/shard_map/ar,br->ab/dot_general | solution.py:55
  221.4 2.8 copy.55
  224.2 8.9 %pad_maximum_fusion.1 = f32[128,8192]{0,1:T(8,128)} fusion(f32[1,8192]{0,1:T(8,128)} %copy.55, f32[1,8192]{0,1:T(8,128)} %copy.54, f32[126,8192]{0,1:T(8,128)} %bitcast.40), kind=kLoop, calls=%fused_computation.20 | loop fusion | flops 2097152 | bytes 8388608 | tf_op jit(solution)/shard_map/concatenate | solution.py:51
  233.1 135.0 %all-reduce.5.cloned.1.call-done = f32[128,128]{0,1:T(8,128)} async-done(((f32[128,128]{0,1:T(8,128)}), f32[128,128]{0,1:T(8,128)}) %all-reduce.5.cloned.1.call-update) | async-done | bytes 65552 | tf_op jit(solution)/shard_map/psum | solution.py:56
  369.9 11.7 %cholesky.16 = f32[128,128]{1,0:T(8,128)S(1)} custom-call(f32[128,128]{1,0:T(8,128)S(1)} %fusion.53), custom_call_target="Cholesky" | custom-call | tf_op jit(solution)/shard_map/jit(cholesky)/cholesky | solution.py:57
  382.9 9.8 %custom-call.6 = f32[1,128,128]{1,2,0:T(8,128)S(1)} custom-call(f32[1,128,128]{2,1,0:T(8,128)S(1)} %get-tuple-element.26), custom_call_target="InvertDiagBlocksLowerTriangular" | custom-call | tf_op jit(solution)/shard_map/triangular_solve | solution.py:58
  392.7 5.7 %fusion.51 = f32[128,8,8,128]{3,0,2,1:T(8,128)S(1)} fusion(f32[8,8,128,128]{3,2,1,0:T(8,128)} %bitcast.41, f32[1,128,128]{1,2,0:T(8,128)S(1)} %custom-call.6), kind=kOutput, calls=%fused_computation.88 | convolution fusion | flops 1610612736 | bytes 8454144 | tf_op jit(solution)/shard_map/triangular_solve | solution.py:58
  398.4 4.4 %copy.57 = f32[128,8,8,128]{3,2,1,0:T(8,128)} copy(f32[128,8,8,128]{3,0,2,1:T(8,128)S(1)} %fusion.51) | data formatting | bytes 8388608
  (35 shorter events, 14.2 us)
Async XLA Ops:
  7.2 360.9 %all-reduce.5.cloned.1.call-start = ((), (), s32[]{:S(2)}) async-start(), calls=%async_computation | async-start | bytes 131072 | tf_op jit(solution)/shard_map/psum | solution.py:56
  7.2 17.2 %copy-start = (f32[16,32,1536]{2,1,0:T(8,128)S(1)}, f32[16,32,1536]{2,1,0:T(8,128)}, u32[]{:S(2)}) copy-start(f32[16,32,1536]{2,1,0:T(8,128)} %param.4) | copy-start | bytes 9437188
  7.2 17.2 %copy-start.1 = (f32[16,32,1536]{2,1,0:T(8,128)S(1)}, f32[16,32,1536]{2,1,0:T(8,128)}, u32[]{:S(2)}) copy-start(f32[16,32,1536]{2,1,0:T(8,128)} %param.3) | copy-start | bytes 9437188
  8.7 11.9 %collective-permute-start = (f32[2,1,32,1536]{3,2,1,0:T(8,128)S(1)}, f32[2,1,32,1536]{3,2,1,0:T(8,128)S(1)}, u32[]{:S(2)}, u32[]{:S(2)}) collective-permute-start(f32[2,1,32,1536]{3,2,1,0:T(8,128)S(1)} %get-tuple-element.19), channel_id=1, source_target_pairs={{0,8},{8,16},{16,24},{24,32},{32,40},{40,48},{48,56},{56,64},{64,7... | collective-permute-start | bytes 1179656 | tf_op jit(solution)/shard_map/ppermute | solution.py:12
  12.8 11.6 %collective-permute-start.1 = (f32[2,1,32,1536]{3,2,1,0:T(8,128)S(1)}, f32[2,1,32,1536]{3,2,1,0:T(8,128)S(1)}, u32[]{:S(2)}, u32[]{:S(2)}) collective-permute-start(f32[2,1,32,1536]{3,2,1,0:T(8,128)S(1)} %get-tuple-element.20), channel_id=1, source_target_pairs={{8,0},{16,8},{24,16},{32,24},{40,32},{48,40},{56,48},{64,56},{72,6... | collective-permute-start | bytes 1179656 | tf_op jit(solution)/shard_map/ppermute | solution.py:15
  24.8 8.1 %collective-permute-start.2 = (f32[2,18,1,1536]{3,2,1,0:T(1,128)S(1)}, f32[2,18,1,1536]{3,2,1,0:T(1,128)S(1)}, u32[]{:S(2)}, u32[]{:S(2)}) collective-permute-start(f32[2,18,1,1536]{3,2,1,0:T(1,128)S(1)} %get-tuple-element.17), channel_id=1, source_target_pairs={{0,1},{1,2},{2,3},{3,4},{4,5},{5,6},{6,7},{8,9},{9,10},{10,11},{11... | collective-permute-start | bytes 663560 | tf_op jit(solution)/shard_map/ppermute | solution.py:12
  30.1 7.3 %collective-permute-start.3 = (f32[2,18,1,1536]{3,2,1,0:T(1,128)S(1)}, f32[2,18,1,1536]{3,2,1,0:T(1,128)S(1)}, u32[]{:S(2)}, u32[]{:S(2)}) collective-permute-start(f32[2,18,1,1536]{3,2,1,0:T(1,128)S(1)} %get-tuple-element.18), channel_id=1, source_target_pairs={{1,0},{2,1},{3,2},{4,3},{5,4},{6,5},{7,6},{9,8},{10,9},{11,10},{12... | collective-permute-start | bytes 663560 | tf_op jit(solution)/shard_map/ppermute | solution.py:15
  71.5 15.7 %copy-start.2 = (f32[126,8,8,128]{3,2,1,0:T(8,128)S(1)}, f32[126,8,8,128]{3,2,1,0:T(8,128)}, u32[]{:S(2)}) copy-start(f32[126,8,8,128]{3,2,1,0:T(8,128)} %param.5) | copy-start | bytes 12386308
  71.6 6.7 %collective-permute-start.4 = (f32[1,32,1536]{2,1,0:T(8,128)S(1)}, f32[1,32,1536]{2,1,0:T(8,128)S(1)}, u32[]{:S(2)}, u32[]{:S(2)}) collective-permute-start(f32[1,32,1536]{2,1,0:T(8,128)S(1)} %get-tuple-element.24), channel_id=1, source_target_pairs={{8,0},{16,8},{24,16},{32,24},{40,32},{48,40},{56,48},{64,56},{72,6... | collective-permute-start | bytes 589832 | tf_op jit(solution)/shard_map/ppermute | solution.py:15
  73.1 6.6 %collective-permute-start.5 = (f32[1,32,1536]{2,1,0:T(8,128)S(1)}, f32[1,32,1536]{2,1,0:T(8,128)S(1)}, u32[]{:S(2)}, u32[]{:S(2)}) collective-permute-start(f32[1,32,1536]{2,1,0:T(8,128)S(1)} %get-tuple-element.23), channel_id=1, source_target_pairs={{0,8},{8,16},{16,24},{24,32},{32,40},{40,48},{48,56},{56,64},{64,7... | collective-permute-start | bytes 589832 | tf_op jit(solution)/shard_map/ppermute | solution.py:12
  80.6 66.5 %collective-permute-start.6 = (f32[18,1,1536]{2,0,1:T(8,128)}, f32[18,1,1536]{2,0,1:T(8,128)}, u32[]{:S(2)}, u32[]{:S(2)}) collective-permute-start(f32[18,1,1536]{2,0,1:T(8,128)} %copy.42), channel_id=1, source_target_pairs={{1,0},{2,1},{3,2},{4,3},{5,4},{6,5},{7,6},{9,8},{10,9},{11,10},{12... | collective-permute-start | bytes 331784 | tf_op jit(solution)/shard_map/ppermute | solution.py:15
  83.1 65.0 %collective-permute-start.7 = (f32[18,1,1536]{2,0,1:T(8,128)}, f32[18,1,1536]{2,0,1:T(8,128)}, u32[]{:S(2)}, u32[]{:S(2)}) collective-permute-start(f32[18,1,1536]{2,0,1:T(8,128)} %copy.44), channel_id=1, source_target_pairs={{0,1},{1,2},{2,3},{3,4},{4,5},{5,6},{6,7},{8,9},{9,10},{10,11},{11... | collective-permute-start | bytes 331784 | tf_op jit(solution)/shard_map/ppermute | solution.py:12
  148.1 5.9 %slice-start = ((s8[4423680]{0:T(1024)(128)(4,1)}), s8[4194304]{0:T(1024)(128)(4,1)S(1)}, s32[]{:S(2)}) async-start(s8[4423680]{0:T(1024)(128)(4,1)} %bitcast.32), calls=%async_computation.1 | async-start | bytes 8388608
  149.3 4.7 %slice-start.1 = ((s8[4423680]{0:T(1024)(128)(4,1)}), s8[229376]{0:T(1024)(128)(4,1)S(1)}, s32[]{:S(2)}) async-start(s8[4423680]{0:T(1024)(128)(4,1)} %bitcast.32), calls=%async_computation.2 | async-start | bytes 458752
  210.8 2.8 copy-start.3
Sparse Core Ops, SparseCore 0:
  221.5 146.5 all-reduce.4
where the time goes:
time: 419 us; the launch traced here: 411 us
  waiting for transfers between devices  153 us (37%)
  local copies, waits for them, and re-layouts  123 us (29%)
  other arithmetic  82.1 us (20%)
  starting transfers between devices  24.2 us (6%)
  between operations  14.5 us (3%)
  matrix products  13.4 us (3%)
    psum x1, waiting for transfers between devices, body(): total = lax.psum(gram, ('gx', 'gy'))  135 us
    reshape x2, local copies, waits for them, and re-layouts, sample(): return field.reshape(a // 2, 2, b // 4, 4, c // 12, 12)[:, 0, :, 0, :, 0]  77.3 us
    add x2, other arithmetic, advance(): return centre + change  41.3 us
    ppermute x4, starting transfers between devices, extended(): lax.ppermute(lax.slice_in_dim(block, block.shape[dim] - width, None, axis...  17.4 us
    unnamed x17, local copies, waits for them, and re-layouts  15.8 us
    another operation x3, other arithmetic, body(): factor = jnp.linalg.cholesky(total).T  12.4 us
    concatenate x3, local copies, waits for them, and re-layouts, body(): jnp.concatenate([history, sample(first)[None], sample(second)[None]], 0)  12.1 us
    another operation x1, other arithmetic, body(): lax.linalg.triangular_solve(factor.T, block, left_side=True, lower=True)  9.81 us
  transfers between devices with their start and end apart: 9, of which 7 were waited for; matrix products, arithmetic and copies ran while one was open for 18% of the time, Pallas kernels for 0%

commit v1 on v0

--- a/solution.py
+++ b/solution.py
@@ -53,7 +53,7 @@
     block = block.reshape(shape[0], -1)
     rows_all = block.shape[1] * lax.axis_size("gx") * lax.axis_size("gy")
     gram = jnp.einsum("ar,br->ab", block, block, precision=lax.Precision.HIGHEST) / rows_all
-    total = lax.psum(gram, ("gx", "gy"))
+    total = jnp.sum(lax.all_gather(gram, ("gx", "gy")), axis=0)
     factor = jnp.linalg.cholesky(total).T
     basis = lax.linalg.triangular_solve(factor.T, block, left_side=True, lower=True)
     return (second, basis.reshape(shape), factor)

time: 419 us -> 352 us (0.84)
  waiting for transfers between devices: 153 us -> 75.6 us
  local copies, waits for them, and re-layouts: 123 us -> 132 us
    psum x1 -> x0, waiting for transfers between devices: 135 us -> none  [body(): total = lax.psum(gram, ('gx', 'gy'))]
    all_gather x0 -> x1, waiting for transfers between devices: none -> 57.4 us  [body(): total = jnp.sum(lax.all_gather(gram, ('gx', 'gy')), axis=0)]
    unnamed x17, local copies, waits for them, and re-layouts: 15.8 us -> 26.9 us
  transfers between devices with their start and end apart: 9 -> 9, of which waited for: 7 -> 7; matrix products, arithmetic and copies ran while one was open for 18% -> 21% of each run, Pallas kernels for 0% -> 0%
where the time goes in v1:
time: 352 us; the launch traced here: 345 us
  local copies, waits for them, and re-layouts  132 us (38%)
  other arithmetic  85 us (24%)
  waiting for transfers between devices  75.6 us (21%)
  starting transfers between devices  24.5 us (7%)
  between operations  14.5 us (4%)
  matrix products  13.4 us (4%)
    reshape x2, local copies, waits for them, and re-layouts, sample(): return field.reshape(a // 2, 2, b // 4, 4, c // 12, 12)[:, 0, :, 0, :, 0]  77.3 us
    all_gather x1, waiting for transfers between devices, body(): total = jnp.sum(lax.all_gather(gram, ('gx', 'gy')), axis=0)  57.4 us
    add x2, other arithmetic, advance(): return centre + change  41.3 us
    unnamed x17, local copies, waits for them, and re-layouts  26.9 us
    ppermute x4, starting transfers between devices, extended(): lax.ppermute(lax.slice_in_dim(block, block.shape[dim] - width, None, axis...  17.8 us
    another operation x3, other arithmetic, body(): factor = jnp.linalg.cholesky(total).T  12.4 us
    concatenate x3, local copies, waits for them, and re-layouts, body(): jnp.concatenate([history, sample(first)[None], sample(second)[None]], 0)  10.7 us
    another operation x1, other arithmetic, body(): lax.linalg.triangular_solve(factor.T, block, left_side=True, lower=True)  9.81 us
  transfers between devices with their start and end apart: 9, of which 7 were waited for; matrix products, arithmetic and copies ran while one was open for 21% of the time, Pallas kernels for 0%

profile of v1, /device:TPU:1, one launch (start us, length us, event | category | flops | bytes accessed | tf_op | source)
XLA Modules:
  0.0 345.3 jit_solution(2317431896076769000)
XLA Ops:
  8.7 4.2 %collective-permute-start = (f32[2,1,32,1536]{3,2,1,0:T(8,128)S(1)}, f32[2,1,32,1536]{3,2,1,0:T(8,128)S(1)}, u32[]{:S(2)}, u32[]{:S(2)}) collective-permute-start(f32[2,1,32,1536]{3,2,1,0:T(8,128)S(1)} %get-tuple-element.19), channel_id=1, source_target_pairs={{0,8},{8,16},{16,24},{24,32},{32,40},{40,48},{48,56},{56,64},{64,7... | collective-permute-start | bytes 1179656 | tf_op jit(solution)/shard_map/ppermute | solution.py:12
  14.1 6.5 %collective-permute-done = f32[2,1,32,1536]{3,2,1,0:T(8,128)S(1)} collective-permute-done((f32[2,1,32,1536]{3,2,1,0:T(8,128)S(1)}, f32[2,1,32,1536]{3,2,1,0:T(8,128)S(1)}, u32[]{:S(2)}, u32[]{:S(2)}) %collective-permute-start) | collective-permute-done | bytes 393248 | tf_op jit(solution)/shard_map/ppermute | solution.py:12
  20.6 3.9 %collective-permute-done.1 = f32[2,1,32,1536]{3,2,1,0:T(8,128)S(1)} collective-permute-done((f32[2,1,32,1536]{3,2,1,0:T(8,128)S(1)}, f32[2,1,32,1536]{3,2,1,0:T(8,128)S(1)}, u32[]{:S(2)}, u32[]{:S(2)}) %collective-permute-start.1) | collective-permute-done | bytes 393248 | tf_op jit(solution)/shard_map/ppermute | solution.py:15
  24.8 5.2 %collective-permute-start.2 = (f32[2,18,1,1536]{3,2,1,0:T(1,128)S(1)}, f32[2,18,1,1536]{3,2,1,0:T(1,128)S(1)}, u32[]{:S(2)}, u32[]{:S(2)}) collective-permute-start(f32[2,18,1,1536]{3,2,1,0:T(1,128)S(1)} %get-tuple-element.17), channel_id=1, source_target_pairs={{0,1},{1,2},{2,3},{3,4},{4,5},{5,6},{6,7},{8,9},{9,10},{10,11},{11... | collective-permute-start | bytes 663560 | tf_op jit(solution)/shard_map/ppermute | solution.py:12
  30.1 1.9 collective-permute-start.3
  32.9 4.4 %collective-permute-done.3 = f32[2,18,1,1536]{3,2,1,0:T(1,128)S(1)} collective-permute-done((f32[2,18,1,1536]{3,2,1,0:T(1,128)S(1)}, f32[2,18,1,1536]{3,2,1,0:T(1,128)S(1)}, u32[]{:S(2)}, u32[]{:S(2)}) %collective-permute-start.3) | collective-permute-done | bytes 221216 | tf_op jit(solution)/shard_map/ppermute | solution.py:15
  37.3 1.7 pad_maximum_fusion
  39.0 4.2 %slice_bitcast_fusion = (f32[18,34,1536]{2,1,0:T(8,128)}, f32[18,34,1536]{2,1,0:T(8,128)}) fusion(f32[2,18,34,1536]{3,2,1,0:T(8,128)S(1)} %pad_maximum_fusion), kind=kLoop, calls=%fused_computation.12 | loop fusion | bytes 15040512 | tf_op jit(solution)/shard_map/squeeze | solution.py:47
  43.2 28.3 %fusion.15 = f32[16,32,1536]{2,1,0:T(8,128)S(1)} fusion(f32[18,34,1536]{2,1,0:T(8,128)} %get-tuple-element.16, f32[18,34,1536]{2,1,0:T(8,128)} %get-tuple-element.15), kind=kLoop, calls=%fused_computation.29 | loop fusion | flops 23592960 | bytes 43450368 | tf_op jit(solution)/shard_map/add | solution.py:36
  73.1 4.0 %collective-permute-start.5 = (f32[1,32,1536]{2,1,0:T(8,128)S(1)}, f32[1,32,1536]{2,1,0:T(8,128)S(1)}, u32[]{:S(2)}, u32[]{:S(2)}) collective-permute-start(f32[1,32,1536]{2,1,0:T(8,128)S(1)} %get-tuple-element.23), channel_id=1, source_target_pairs={{0,8},{8,16},{16,24},{24,32},{32,40},{40,48},{48,56},{56,64},{64,7... | collective-permute-start | bytes 589832 | tf_op jit(solution)/shard_map/ppermute | solution.py:12
  80.6 1.9 collective-permute-start.6
  83.1 4.4 %collective-permute-start.7 = (f32[18,1,1536]{2,0,1:T(8,128)}, f32[18,1,1536]{2,0,1:T(8,128)}, u32[]{:S(2)}, u32[]{:S(2)}) collective-permute-start(f32[18,1,1536]{2,0,1:T(8,128)} %copy.41), channel_id=1, source_target_pairs={{0,1},{1,2},{2,3},{3,4},{4,5},{5,6},{6,7},{8,9},{9,10},{10,11},{11... | collective-permute-start | bytes 331784 | tf_op jit(solution)/shard_map/ppermute | solution.py:12
  87.6 4.4 %copy.47 = f32[126,8,8,128]{3,0,2,1:T(8,128)} copy(f32[126,8,8,128]{3,2,1,0:T(8,128)S(1)} %copy-done.2) | data formatting | bytes 8257536 | tf_op args[2]
  92.0 38.1 %reshape.29 = f32[8,2,8,4,128,12]{5,4,3,2,1,0:T(8,128)} reshape(f32[16,32,1536]{2,1,0:T(8,128)S(1)} %fusion.15) | data formatting | bytes 6291456 | tf_op jit(solution)/shard_map/reshape | solution.py:41
  130.1 4.7 %slice.184 = f32[8,1,8,1,128,1]{5,4,3,2,1,0:T(8,128)} slice(f32[8,2,8,4,128,12]{5,4,3,2,1,0:T(8,128)} %reshape.29), slice={[0:8], [0:1], [0:8], [0:1], [0:128], [0:1]} | slice | bytes 65536 | tf_op jit(solution)/shard_map/slice | solution.py:41
  134.8 3.4 copy.59
  140.5 4.7 %select_maximum_fusion = f32[18,34,1538]{2,1,0:T(8,128)S(1)} fusion(f32[18,1,1536]{2,1,0:T(1,128)S(1)} %copy.40, f32[18,1,1536]{2,1,0:T(1,128)S(1)} %copy.42, f32[1,32,1536]{2,1,0:T(8,128)S(1)} %collective-permute-done.4, f32[16,32,1536]{2,1,0:T(8,128)S(1)} %fusion.15, f32[1,32,1536]{2,1,0:T(8,128)S(1)} %collective-permute-done.5), kind=kLoop, calls=%fused_computation.3 | loop fusion | flops 11295072 | bytes 7525152 | tf_op jit(solution)/shard_map/concatenate | solution.py:16
  145.2 12.9 %fusion.20 = f32[16,32,1536]{2,1,0:T(8,128)} fusion(f32[16,32,1536]{2,1,0:T(8,128)S(1)} %fusion.15, f32[18,34,1538]{2,1,0:T(8,128)S(1)} %select_maximum_fusion, f32[18,1,1536]{2,1,0:T(1,128)S(1)} %copy.42, f32[1,32,1536]{2,1,0:T(8,128)S(1)} %collective-permute-done.4, f32[1,32,1536]{2,1,0:T(8,128)S(1)} %collective-permute-done.5, ...), kind=kLoop, calls=%fused_computation.35 | loop fusion | flops 29884416 | bytes 33349632 | tf_op jit(solution)/shard_map/add | solution.py:36
  158.1 39.1 %reshape.30 = f32[8,2,8,4,128,12]{5,4,3,2,1,0:T(8,128)} reshape(f32[16,32,1536]{2,1,0:T(8,128)} %fusion.20) | data formatting | bytes 6291456 | tf_op jit(solution)/shard_map/reshape | solution.py:41
  197.3 4.7 %slice.185 = f32[8,1,8,1,128,1]{5,4,3,2,1,0:T(8,128)} slice(f32[8,2,8,4,128,12]{5,4,3,2,1,0:T(8,128)} %reshape.30), slice={[0:8], [0:1], [0:8], [0:1], [0:128], [0:1]} | slice | bytes 65536 | tf_op jit(solution)/shard_map/slice | solution.py:41
  202.0 13.9 %copy.60 = f32[8,1,8,1,128,1]{4,2,0,5,3,1:T(8,128)S(1)} copy(f32[8,1,8,1,128,1]{5,4,3,2,1,0:T(8,128)} %slice.185) | data formatting | bytes 65536
  215.9 7.7 %fusion.48 = f32[128,128]{1,0:T(8,128)} fusion(f32[1,8,8,128]{3,0,2,1:T(1,128)S(1)} %bitcast.48, f32[1,8,8,128]{3,0,2,1:T(1,128)S(1)} %bitcast.46, f32[126,8,8,128]{3,0,2,1:T(8,128)} %copy.47), kind=kOutput, calls=%fused_computation.78 | convolution fusion | flops 1612726272 | bytes 4259840 | tf_op jit(solution)/shard_map/ar,br->ab/dot_general | solution.py:55
  223.6 5.5 %copy.58 = f32[126,8,8,128]{0,3,2,1:T(8,128)} copy(f32[126,8,8,128]{3,2,1,0:T(8,128)} %param.5) | data formatting | bytes 8257536 | tf_op jit(solution)/shard_map/concatenate | solution.py:51
  229.0 2.6 copy.50
  231.6 2.7 copy.51
  234.3 8.9 %pad_maximum_fusion.1 = f32[128,8192]{0,1:T(8,128)} fusion(f32[1,8192]{0,1:T(8,128)} %copy.51, f32[1,8192]{0,1:T(8,128)} %copy.50, f32[126,8192]{0,1:T(8,128)} %bitcast.44), kind=kLoop, calls=%fused_computation.20 | loop fusion | flops 2097152 | bytes 8388608 | tf_op jit(solution)/shard_map/concatenate | solution.py:51
  243.2 57.4 %all-gather.3.cloned.1.call-done = f32[16384,128]{1,0:T(8,128)} async-done(((f32[128,128]{1,0:T(8,128)}), f32[16384,128]{1,0:T(8,128)}) %all-gather.3.cloned.1.call-update) | async-done | bytes 8388624 | tf_op jit(solution)/shard_map/all_gather | solution.py:56
  300.6 3.8 %reduce_sum.9 = f32[128,128]{1,0:T(8,128)S(1)} reduce(f32[128,128,128]{2,1,0:T(8,128)} %bitcast.45, f32[]{:T(128)} %constant.44.clone.1), dimensions={0}, to_apply=%region_0.1 | reduce | flops 2080768 | bytes 8454148 | tf_op jit(solution)/shard_map/reduce_sum | solution.py:56
  304.5 11.7 %cholesky.16 = f32[128,128]{1,0:T(8,128)S(1)} custom-call(f32[128,128]{1,0:T(8,128)S(1)} %fusion.53), custom_call_target="Cholesky" | custom-call | tf_op jit(solution)/shard_map/jit(cholesky)/cholesky | solution.py:57
  317.5 9.8 %custom-call.6 = f32[1,128,128]{1,2,0:T(8,128)S(1)} custom-call(f32[1,128,128]{2,1,0:T(8,128)S(1)} %get-tuple-element.26), custom_call_target="InvertDiagBlocksLowerTriangular" | custom-call | tf_op jit(solution)/shard_map/triangular_solve | solution.py:58
  327.4 5.7 %fusion.51 = f32[128,8,8,128]{3,0,2,1:T(8,128)S(1)} fusion(f32[8,8,128,128]{3,2,1,0:T(8,128)} %bitcast.43, f32[1,128,128]{1,2,0:T(8,128)S(1)} %custom-call.6), kind=kOutput, calls=%fused_computation.88 | convolution fusion | flops 1610612736 | bytes 8454144 | tf_op jit(solution)/shard_map/triangular_solve | solution.py:58
  333.0 4.4 %copy.53 = f32[128,8,8,128]{3,2,1,0:T(8,128)} copy(f32[128,8,8,128]{3,0,2,1:T(8,128)S(1)} %fusion.51) | data formatting | bytes 8388608
  (36 shorter events, 14.1 us)
Async XLA Ops:
  7.2 293.4 %all-gather.3.cloned.1.call-start = ((), (), s32[]{:S(2)}) async-start(), calls=%async_computation | async-start | bytes 8454144 | tf_op jit(solution)/shard_map/all_gather | solution.py:56
  7.2 17.2 %copy-start = (f32[16,32,1536]{2,1,0:T(8,128)S(1)}, f32[16,32,1536]{2,1,0:T(8,128)}, u32[]{:S(2)}) copy-start(f32[16,32,1536]{2,1,0:T(8,128)} %param.4) | copy-start | bytes 9437188
  7.2 17.2 %copy-start.1 = (f32[16,32,1536]{2,1,0:T(8,128)S(1)}, f32[16,32,1536]{2,1,0:T(8,128)}, u32[]{:S(2)}) copy-start(f32[16,32,1536]{2,1,0:T(8,128)} %param.3) | copy-start | bytes 9437188
  8.7 11.9 %collective-permute-start = (f32[2,1,32,1536]{3,2,1,0:T(8,128)S(1)}, f32[2,1,32,1536]{3,2,1,0:T(8,128)S(1)}, u32[]{:S(2)}, u32[]{:S(2)}) collective-permute-start(f32[2,1,32,1536]{3,2,1,0:T(8,128)S(1)} %get-tuple-element.19), channel_id=1, source_target_pairs={{0,8},{8,16},{16,24},{24,32},{32,40},{40,48},{48,56},{56,64},{64,7... | collective-permute-start | bytes 1179656 | tf_op jit(solution)/shard_map/ppermute | solution.py:12
  12.8 11.6 %collective-permute-start.1 = (f32[2,1,32,1536]{3,2,1,0:T(8,128)S(1)}, f32[2,1,32,1536]{3,2,1,0:T(8,128)S(1)}, u32[]{:S(2)}, u32[]{:S(2)}) collective-permute-start(f32[2,1,32,1536]{3,2,1,0:T(8,128)S(1)} %get-tuple-element.20), channel_id=1, source_target_pairs={{8,0},{16,8},{24,16},{32,24},{40,32},{48,40},{56,48},{64,56},{72,6... | collective-permute-start | bytes 1179656 | tf_op jit(solution)/shard_map/ppermute | solution.py:15
  24.8 8.1 %collective-permute-start.2 = (f32[2,18,1,1536]{3,2,1,0:T(1,128)S(1)}, f32[2,18,1,1536]{3,2,1,0:T(1,128)S(1)}, u32[]{:S(2)}, u32[]{:S(2)}) collective-permute-start(f32[2,18,1,1536]{3,2,1,0:T(1,128)S(1)} %get-tuple-element.17), channel_id=1, source_target_pairs={{0,1},{1,2},{2,3},{3,4},{4,5},{5,6},{6,7},{8,9},{9,10},{10,11},{11... | collective-permute-start | bytes 663560 | tf_op jit(solution)/shard_map/ppermute | solution.py:12
  30.1 7.3 %collective-permute-start.3 = (f32[2,18,1,1536]{3,2,1,0:T(1,128)S(1)}, f32[2,18,1,1536]{3,2,1,0:T(1,128)S(1)}, u32[]{:S(2)}, u32[]{:S(2)}) collective-permute-start(f32[2,18,1,1536]{3,2,1,0:T(1,128)S(1)} %get-tuple-element.18), channel_id=1, source_target_pairs={{1,0},{2,1},{3,2},{4,3},{5,4},{6,5},{7,6},{9,8},{10,9},{11,10},{12... | collective-permute-start | bytes 663560 | tf_op jit(solution)/shard_map/ppermute | solution.py:15
  71.5 16.0 %copy-start.2 = (f32[126,8,8,128]{3,2,1,0:T(8,128)S(1)}, f32[126,8,8,128]{3,2,1,0:T(8,128)}, u32[]{:S(2)}) copy-start(f32[126,8,8,128]{3,2,1,0:T(8,128)} %param.5) | copy-start | bytes 12386308
  71.6 6.7 %collective-permute-start.4 = (f32[1,32,1536]{2,1,0:T(8,128)S(1)}, f32[1,32,1536]{2,1,0:T(8,128)S(1)}, u32[]{:S(2)}, u32[]{:S(2)}) collective-permute-start(f32[1,32,1536]{2,1,0:T(8,128)S(1)} %get-tuple-element.24), channel_id=1, source_target_pairs={{8,0},{16,8},{24,16},{32,24},{40,32},{48,40},{56,48},{64,56},{72,6... | collective-permute-start | bytes 589832 | tf_op jit(solution)/shard_map/ppermute | solution.py:15
  73.1 6.6 %collective-permute-start.5 = (f32[1,32,1536]{2,1,0:T(8,128)S(1)}, f32[1,32,1536]{2,1,0:T(8,128)S(1)}, u32[]{:S(2)}, u32[]{:S(2)}) collective-permute-start(f32[1,32,1536]{2,1,0:T(8,128)S(1)} %get-tuple-element.23), channel_id=1, source_target_pairs={{0,8},{8,16},{16,24},{24,32},{32,40},{40,48},{48,56},{56,64},{64,7... | collective-permute-start | bytes 589832 | tf_op jit(solution)/shard_map/ppermute | solution.py:12
  80.6 57.7 %collective-permute-start.6 = (f32[18,1,1536]{2,0,1:T(8,128)}, f32[18,1,1536]{2,0,1:T(8,128)}, u32[]{:S(2)}, u32[]{:S(2)}) collective-permute-start(f32[18,1,1536]{2,0,1:T(8,128)} %copy.39), channel_id=1, source_target_pairs={{1,0},{2,1},{3,2},{4,3},{5,4},{6,5},{7,6},{9,8},{10,9},{11,10},{12... | collective-permute-start | bytes 331784 | tf_op jit(solution)/shard_map/ppermute | solution.py:15
  83.1 56.1 %collective-permute-start.7 = (f32[18,1,1536]{2,0,1:T(8,128)}, f32[18,1,1536]{2,0,1:T(8,128)}, u32[]{:S(2)}, u32[]{:S(2)}) collective-permute-start(f32[18,1,1536]{2,0,1:T(8,128)} %copy.41), channel_id=1, source_target_pairs={{0,1},{1,2},{2,3},{3,4},{4,5},{5,6},{6,7},{8,9},{9,10},{10,11},{11... | collective-permute-start | bytes 331784 | tf_op jit(solution)/shard_map/ppermute | solution.py:12
  139.3 5.9 %slice-start = ((s8[4423680]{0:T(1024)(128)(4,1)}), s8[4194304]{0:T(1024)(128)(4,1)S(1)}, s32[]{:S(2)}) async-start(s8[4423680]{0:T(1024)(128)(4,1)} %bitcast.35), calls=%async_computation.1 | async-start | bytes 8388608
  140.5 4.7 %slice-start.1 = ((s8[4423680]{0:T(1024)(128)(4,1)}), s8[229376]{0:T(1024)(128)(4,1)S(1)}, s32[]{:S(2)}) async-start(s8[4423680]{0:T(1024)(128)(4,1)} %bitcast.35), calls=%async_computation.2 | async-start | bytes 458752
  202.0 13.9 %copy-start.3 = (f32[8,1,8,1,128,1]{4,2,0,5,3,1:T(8,128)S(1)}, f32[8,1,8,1,128,1]{4,2,0,5,3,1:T(8,128)}, u32[]{:S(2)}) copy-start(f32[8,1,8,1,128,1]{4,2,0,5,3,1:T(8,128)} %copy.59) | copy-start | bytes 98308
Sparse Core Ops, SparseCore 0:
  223.7 76.8 all-gather.2
